TPU v7x, 256 devices: a whole 4x4x8 slice. The times are simulated.
256 devices in a mesh: dom: 32 (over y_hi, z, core), col: 8 (over x, y_lo).
Axes of the slice: x: 4, y: 4 (y_hi: 2, y_lo: 2; y = y_hi * 2 + y_lo), z: 8, core: 2. Of those that a mesh axis runs over, the one named last changes fastest.
Arguments:
- tmat: bfloat16 [131072, 4096], P('dom', 'col'), may hold values from -6 to 6
- stored_mass_blocks: bfloat16 [8192, 128, 128], P('dom'), may hold values from -0.0007324219 to 0.0007324219
- block_index: int32 [8192, 2], P('dom'), may hold values from 0 to 35, as said below
- live_block_count: int32 [32], P('dom'), may hold values from 36 to 256, as said below
- send_rows: int32 [64, 256], P('dom'), may hold values from 0 to 4095, as said below
Outputs:
- reduced: float32 [512, 4096], P('dom', 'col')
Inputs may be any that keep to these rules, and one draw needn't show every extreme that they name: `block_index`: row entries lie in 0 to 31 and column entries in 0 to 35. In each partition's list slot k < 32 is block (k, k), and slot 32 + m for m < 4 has block column 32 + m. `live_block_count`: some partition uses all 256 slots in every draw. `send_rows`: the 256 rows in each list are distinct local row numbers of the sending partition.
All inputs are finite; a program needn't handle non-finite values.
Results may differ from a plain program's by a relative error of at most 0.0029.
Values may be sent and summed in bfloat16 or wider, within the bound.
A program may use at most 128 MiB of HBM per device.

v0:
```python
import jax
import jax.numpy as jnp
from jax import lax
from jax.sharding import PartitionSpec as P


def passed_along(block, axis, distance):
    devices = range(lax.axis_size(axis))
    route = [(i - distance, i) for i in devices if i - distance in devices]
    return lax.ppermute(block, axis, route)


def broadcast(block, axis, holder):
    block = jnp.where(lax.axis_index(axis) == holder, block, jnp.zeros_like(block))
    return lax.psum(block, axis)


def contract(left, right):
    return lax.dot_general(
        left, right, (((0,), (0,)), ((), ())), preferred_element_type=jnp.float32
    )


def mass_product(panel, stored_mass_blocks, block_index, live_block_count, send_rows):
    rows_dev, width = panel.shape
    bsize = stored_mass_blocks.shape[1]
    nrows_blk = rows_dev // bsize
    slot_number = stored_mass_blocks.shape[0]
    to_lower = jnp.take(panel, send_rows[0], axis=0)
    to_upper = jnp.take(panel, send_rows[1], axis=0)
    from_lower = passed_along(to_upper, "dom", 1)
    from_upper = passed_along(to_lower, "dom", -1)
    extended = jnp.concatenate([panel, from_lower, from_upper], 0).reshape(-1, bsize, width)
    live_flags = (jnp.arange(slot_number) < live_block_count[0]).astype(jnp.float32)
    partition_groups = 4
    partition_group_width = slot_number // partition_groups

    def step(acc, group):
        begin = group * partition_group_width
        blocks = lax.dynamic_slice_in_dim(stored_mass_blocks, begin, partition_group_width, 0)
        columns = lax.dynamic_slice_in_dim(block_index[:, 1], begin, partition_group_width, 0)
        targets = lax.dynamic_slice_in_dim(block_index[:, 0], begin, partition_group_width, 0)
        weights = lax.dynamic_slice_in_dim(live_flags, begin, partition_group_width, 0)
        selected = jnp.take(extended, columns, axis=0)
        prod = jnp.einsum("kab,kbw->kaw", blocks, selected, preferred_element_type=jnp.float32)
        acc = acc.at[targets].add(prod * weights[:, None, None])
        return (acc, None)

    start_acc = jnp.zeros((nrows_blk, bsize, width), jnp.float32)
    summed, _ = lax.scan(step, start_acc, jnp.arange(partition_groups))
    return summed.reshape(rows_dev, width).astype(jnp.bfloat16)


def body(tmat, stored_mass_blocks, block_index, live_block_count, send_rows):
    n_col = lax.axis_size("col")
    n_dom = lax.axis_size("dom")
    panel_width = tmat.shape[1]
    panel = broadcast(tmat, "col", n_col - 1)
    interface_mass_panel = mass_product(
        panel, stored_mass_blocks, block_index, live_block_count, send_rows
    )
    share = panel_width // n_dom
    total = lax.psum(contract(interface_mass_panel, tmat), "dom")
    return lax.dynamic_slice_in_dim(total, lax.axis_index("dom") * share, share, 0)


def solution(mesh):
    return jax.shard_map(
        body,
        mesh=mesh,
        in_specs=(P("dom", "col"), P("dom", None, None), P("dom", None), P("dom"), P("dom", None)),
        out_specs=P("dom", "col"),
        check_vma=False,
    )
```

profile of v0, /device:TPU:33, one launch (start us, length us, event | category | flops | bytes accessed | tf_op | source)
XLA Modules:
  0.0 743.6 jit_solution(13269119770228952049)
XLA Ops:
  6.5 2.2 broadcast_select_fusion
  9.0 190.9 %all-reduce.3.cloned.1.call-done = bf16[4096,512]{1,0:T(8,128)(2,1)} async-done(((bf16[4096,512]{1,0:T(8,128)(2,1)}), bf16[4096,512]{1,0:T(8,128)(2,1)}) %all-reduce.3.cloned.1.call-update) | async-done | bytes 4194320 | tf_op jit(solution)/shard_map/psum | solution.py:15
  199.8 3.9 gather_fusion.1
  203.8 0.1 broadcast_select_fusion.2
  203.9 4.2 collective-permute-start
  208.1 3.9 gather_fusion.2
  212.1 1.9 collective-permute-start.1
  214.8 5.1 collective-permute-done.1
  219.8 4.0 pad_maximum_fusion
  223.8 4.3 broadcast_in_dim.27
  228.1 233.6 %while.10 = (s32[]{:T(128)}, f32[32,128,512]{2,1,0:T(8,128)}, s32[256,2]{0,1:T(2,128)S(1)}, s32[4]{0:T(128)S(1)}, bf16[256,128,128]{2,1,0:T(8,128)(2,1)}, /*inde...) while((s32[]{:T(128)}, f32[32,128,512]{2,1,0:T(8,128)}, ...), condition=%wide.region_3.5_spmd, body=%wide.region_1.0_spmd.sunk | while | flops 1086326400 | bytes 94382912 | solution.py:50
  228.1 0.7 dynamic_slice.38
  229.7 7.9 %gather_fusion = bf16[64,128,512]{2,1,0:T(8,128)(2,1)} fusion(bf16[36,128,512]{2,1,0:T(8,128)(2,1)} %get-tuple-element.142, s32[1024]{0:T(1024)S(1)} %pad_clamp_fusion.4), kind=kCustom, calls=%fused_computation.1.clone.1 | custom fusion | bytes 16777472 | tf_op jit(solution)/shard_map/while/body/eval_jaxpr/jit(_take)/gather | solution.py:44
  237.6 12.2 %convolution_multiply_fusion.2 = f32[64,128,512]{2,1,0:T(8,128)} fusion(f32[64]{0:T(128)S(1)} %dynamic_slice.39, bf16[64,128,512]{2,1,0:T(8,128)(2,1)} %gather_fusion, pred[64]{0:T(512)(128)(4,1)S(1)} %get-tuple-element.114, bf16[256,128,128]{2,1,0:T(8,128)(2,1)} %get-tuple-element.141, s32[]{:T(128)S(6)} %select_n.70), kind=kOutput, calls=%fused_computation.4.clone.1 | convolution fusion | flops 1082130432 | bytes 27263300 | tf_op jit(solution)/shard_map/while/body/eval_jaxpr/kab,kbw->kaw/dot_general | solution.py:45
  249.8 36.9 %scatter_fusion = f32[32,128,512]{2,1,0:T(8,128)} fusion(f32[32,128,512]{2,1,0:T(8,128)} %get-tuple-element.127, s32[64]{0:T(128)S(1)} %fusion.19, f32[64,128,512]{2,1,0:T(8,128)} %convolution_multiply_fusion.2), kind=kCustom, calls=%fused_computation.3.clone.1 | custom fusion | flops 4194304 | bytes 50331904 | tf_op jit(solution)/shard_map/while/body/eval_jaxpr/scatter-add | solution.py:46
  286.7 0.7 dynamic_slice.38
  288.3 7.9 %gather_fusion = bf16[64,128,512]{2,1,0:T(8,128)(2,1)} fusion(bf16[36,128,512]{2,1,0:T(8,128)(2,1)} %get-tuple-element.142, s32[1024]{0:T(1024)S(1)} %pad_clamp_fusion.4), kind=kCustom, calls=%fused_computation.1.clone.1 | custom fusion | bytes 16777472 | tf_op jit(solution)/shard_map/while/body/eval_jaxpr/jit(_take)/gather | solution.py:44
  296.2 12.2 %convolution_multiply_fusion.2 = f32[64,128,512]{2,1,0:T(8,128)} fusion(f32[64]{0:T(128)S(1)} %dynamic_slice.39, bf16[64,128,512]{2,1,0:T(8,128)(2,1)} %gather_fusion, pred[64]{0:T(512)(128)(4,1)S(1)} %get-tuple-element.114, bf16[256,128,128]{2,1,0:T(8,128)(2,1)} %get-tuple-element.141, s32[]{:T(128)S(6)} %select_n.70), kind=kOutput, calls=%fused_computation.4.clone.1 | convolution fusion | flops 1082130432 | bytes 27263300 | tf_op jit(solution)/shard_map/while/body/eval_jaxpr/kab,kbw->kaw/dot_general | solution.py:45
  308.3 36.6 %scatter_fusion = f32[32,128,512]{2,1,0:T(8,128)} fusion(f32[32,128,512]{2,1,0:T(8,128)} %get-tuple-element.127, s32[64]{0:T(128)S(1)} %fusion.19, f32[64,128,512]{2,1,0:T(8,128)} %convolution_multiply_fusion.2), kind=kCustom, calls=%fused_computation.3.clone.1 | custom fusion | flops 4194304 | bytes 50331904 | tf_op jit(solution)/shard_map/while/body/eval_jaxpr/scatter-add | solution.py:46
  344.9 0.7 dynamic_slice.38
  346.5 7.9 %gather_fusion = bf16[64,128,512]{2,1,0:T(8,128)(2,1)} fusion(bf16[36,128,512]{2,1,0:T(8,128)(2,1)} %get-tuple-element.142, s32[1024]{0:T(1024)S(1)} %pad_clamp_fusion.4), kind=kCustom, calls=%fused_computation.1.clone.1 | custom fusion | bytes 16777472 | tf_op jit(solution)/shard_map/while/body/eval_jaxpr/jit(_take)/gather | solution.py:44
  354.4 12.2 %convolution_multiply_fusion.2 = f32[64,128,512]{2,1,0:T(8,128)} fusion(f32[64]{0:T(128)S(1)} %dynamic_slice.39, bf16[64,128,512]{2,1,0:T(8,128)(2,1)} %gather_fusion, pred[64]{0:T(512)(128)(4,1)S(1)} %get-tuple-element.114, bf16[256,128,128]{2,1,0:T(8,128)(2,1)} %get-tuple-element.141, s32[]{:T(128)S(6)} %select_n.70), kind=kOutput, calls=%fused_computation.4.clone.1 | convolution fusion | flops 1082130432 | bytes 27263300 | tf_op jit(solution)/shard_map/while/body/eval_jaxpr/kab,kbw->kaw/dot_general | solution.py:45
  366.6 36.8 %scatter_fusion = f32[32,128,512]{2,1,0:T(8,128)} fusion(f32[32,128,512]{2,1,0:T(8,128)} %get-tuple-element.127, s32[64]{0:T(128)S(1)} %fusion.19, f32[64,128,512]{2,1,0:T(8,128)} %convolution_multiply_fusion.2), kind=kCustom, calls=%fused_computation.3.clone.1 | custom fusion | flops 4194304 | bytes 50331904 | tf_op jit(solution)/shard_map/while/body/eval_jaxpr/scatter-add | solution.py:46
  403.4 0.7 dynamic_slice.38
  405.0 7.9 %gather_fusion = bf16[64,128,512]{2,1,0:T(8,128)(2,1)} fusion(bf16[36,128,512]{2,1,0:T(8,128)(2,1)} %get-tuple-element.142, s32[1024]{0:T(1024)S(1)} %pad_clamp_fusion.4), kind=kCustom, calls=%fused_computation.1.clone.1 | custom fusion | bytes 16777472 | tf_op jit(solution)/shard_map/while/body/eval_jaxpr/jit(_take)/gather | solution.py:44
  412.8 12.2 %convolution_multiply_fusion.2 = f32[64,128,512]{2,1,0:T(8,128)} fusion(f32[64]{0:T(128)S(1)} %dynamic_slice.39, bf16[64,128,512]{2,1,0:T(8,128)(2,1)} %gather_fusion, pred[64]{0:T(512)(128)(4,1)S(1)} %get-tuple-element.114, bf16[256,128,128]{2,1,0:T(8,128)(2,1)} %get-tuple-element.141, s32[]{:T(128)S(6)} %select_n.70), kind=kOutput, calls=%fused_computation.4.clone.1 | convolution fusion | flops 1082130432 | bytes 27263300 | tf_op jit(solution)/shard_map/while/body/eval_jaxpr/kab,kbw->kaw/dot_general | solution.py:45
  425.0 36.7 %scatter_fusion = f32[32,128,512]{2,1,0:T(8,128)} fusion(f32[32,128,512]{2,1,0:T(8,128)} %get-tuple-element.127, s32[64]{0:T(128)S(1)} %fusion.19, f32[64,128,512]{2,1,0:T(8,128)} %convolution_multiply_fusion.2), kind=kCustom, calls=%fused_computation.3.clone.1 | custom fusion | flops 4194304 | bytes 50331904 | tf_op jit(solution)/shard_map/while/body/eval_jaxpr/scatter-add | solution.py:46
  461.7 4.2 convert_element_type.10
  465.9 0.4 copy-done
  466.3 3.4 fusion.9
  469.7 265.7 %all-reduce.5.cloned.1.call-done = f32[512,512]{1,0:T(8,128)} async-done(((f32[512,512]{1,0:T(8,128)}), f32[512,512]{1,0:T(8,128)}) %all-reduce.5.cloned.1.call-update) | async-done | bytes 1048592 | tf_op jit(solution)/shard_map/psum | solution.py:63
  735.4 1.4 constant_dynamic-slice_fusion.2
  (40 shorter events, 1.2 us)
Async XLA Ops:
  6.5 2.3 copy-start.2
  6.5 193.3 %all-reduce.3.cloned.1.call-start = ((), (), s32[]{:S(2)}) async-start(), calls=%async_computation | async-start | bytes 8388608 | tf_op jit(solution)/shard_map/psum | solution.py:15
  8.8 726.6 %all-reduce.5.cloned.1.call-start = ((), (), s32[]{:S(2)}) async-start(), calls=%async_computation.1 | async-start | bytes 2097152 | tf_op jit(solution)/shard_map/psum | solution.py:63
  203.9 10.9 %collective-permute-start = (bf16[256,512]{1,0:T(8,128)(2,1)S(1)}, bf16[256,512]{1,0:T(8,128)(2,1)S(1)}, u32[]{:S(2)}, u32[]{:S(2)}) collective-permute-start(bf16[256,512]{1,0:T(8,128)(2,1)S(1)} %broadcast_select_fusion.2), channel_id=1, source_target_pairs={{0,8},{8,16},{16,24},{24,32},{32,40},{40,48},{48,56},{56,64},{64,7... | collective-permute-start | bytes 786440 | tf_op jit(solution)/shard_map/ppermute | solution.py:10
  212.1 7.7 %collective-permute-start.1 = (bf16[256,512]{1,0:T(8,128)(2,1)S(1)}, bf16[256,512]{1,0:T(8,128)(2,1)S(1)}, u32[]{:S(2)}, u32[]{:S(2)}) collective-permute-start(bf16[256,512]{1,0:T(8,128)(2,1)S(1)} %broadcast_select_fusion.1), channel_id=1, source_target_pairs={{8,0},{16,8},{24,16},{32,24},{40,32},{48,40},{56,48},{64,56},{72,6... | collective-permute-start | bytes 786440 | tf_op jit(solution)/shard_map/ppermute | solution.py:10
  214.7 13.4 %copy-start.1 = (s32[256,2]{0,1:T(2,128)S(1)}, s32[256,2]{0,1:T(2,128)}, u32[]{:S(2)}) copy-start(s32[256,2]{0,1:T(2,128)} %param.11) | copy-start | bytes 6148
  461.7 4.6 copy-start
Sparse Core Ops, SparseCore 0:
  10.0 189.7 all-reduce.2
  469.8 265.5 all-reduce.4
where the time goes:
time: 750 us; the launch traced here: 744 us
  waiting for transfers between devices  462 us (62%)
  other arithmetic  158 us (21%)
  matrix products  52 us (7%)
  local copies, waits for them, and re-layouts  48.4 us (6%)
  between operations  14.2 us (2%)
    psum x1, waiting for transfers between devices, body(): total = lax.psum(contract(interface_mass_panel, tmat), 'dom')  266 us
    psum x1, waiting for transfers between devices, broadcast(): return lax.psum(block, axis)  191 us
    scatter-add x4, other arithmetic, step(): acc = acc.at[targets].add(prod * weights[:, None, None])  147 us
    dot_general x4, matrix products, step(): jnp.einsum('kab,kbw->kaw', blocks, selected, preferred_element_type=jnp.f...  48.6 us
    gather x4, local copies, waits for them, and re-layouts, step(): selected = jnp.take(extended, columns, axis=0)  31.5 us
  transfers between devices with their start and end apart: 4, of which 3 were waited for; matrix products, arithmetic and copies ran while one was open for 1% of the time, Pallas kernels for 0%

commit v1 on v0

v1 whole, which is shorter than its diff:
```python
import functools

import jax
import jax.numpy as jnp
from jax import lax
from jax.experimental import pallas as pl
from jax.experimental.pallas import tpu as pltpu
from jax.sharding import PartitionSpec as P

F32 = jnp.float32
BF16 = jnp.bfloat16
BS = 128
W = 512
NB = 32
NS = 256
NPAIR = (NS + NB) // 2
NCH = 4
MC = W // NCH
OFF = 3
PER = 11

TREES = (
    ("00>10", "10>20", "20>21", "21>31", "10>11", "11>01", "20>30"),
    ("00>30", "30>20", "20>10", "30>31", "31>21", "21>11", "31>01"),
    ("00>01", "01>11", "11>21", "21>20", "01>31", "31>30", "11>10"),
)
FIRST = (0, 11, 22, 32)


def column_of(node):
    x, y = int(node[0]), int(node[1])
    return (x + 3) % 4 * 2 + 1 - y


def tree_tables():
    tables = []
    for edges in TREES:
        kids = [[-1, -1] for _ in range(8)]
        depth = [0] * 8
        for edge in edges:
            a, b = (column_of(n) for n in edge.split(">"))
            depth[b] = depth[a] + 1
            kids[a][0 if kids[a][0] < 0 else 1] = b
        tables.append((depth, [k[0] for k in kids], [k[1] for k in kids]))
    return tables


def pick(values, index):
    out = jnp.int32(values[0])
    for i, v in enumerate(values[1:], 1):
        out = jnp.where(index == i, jnp.int32(v), out)
    return out


def product_kernel(slot_ref, colm_ref, start_ref, tmat_ref, low_ref, up_ref, mass_ref, out_ref, ext, acc):
    eye = (
        lax.broadcasted_iota(jnp.int32, (BS, BS), 0) == lax.broadcasted_iota(jnp.int32, (BS, BS), 1)
    ).astype(BF16)

    def turn(block):
        parts = [
            lax.dot_general(
                eye, block[:, g * BS:(g + 1) * BS], (((1,), (1,)), ((), ())), preferred_element_type=F32
            ).astype(BF16)
            for g in range(W // BS)
        ]
        return jnp.concatenate(parts, axis=0)

    def turn_own(c, _):
        ext[c] = turn(tmat_ref[pl.ds(pl.multiple_of(c * BS, BS), BS), :])
        return 0

    lax.fori_loop(0, NB, turn_own, 0)
    for h in range(2):
        ext[NB + h] = turn(low_ref[h * BS:(h + 1) * BS, :])
        ext[NB + 2 + h] = turn(up_ref[h * BS:(h + 1) * BS, :])

    def row(r, _):
        def pair_product(q):
            lhs = jnp.concatenate([ext[colm_ref[2 * q]], ext[colm_ref[2 * q + 1]]], axis=1)
            rhs = jnp.concatenate([mass_ref[slot_ref[2 * q]], mass_ref[slot_ref[2 * q + 1]]], axis=1)
            return lax.dot_general(lhs, rhs, (((1,), (1,)), ((), ())), preferred_element_type=F32)

        begin = start_ref[r]
        acc[...] = pair_product(begin)

        def more(q, _):
            acc[...] += pair_product(q)
            return 0

        lax.fori_loop(begin + 1, start_ref[r + 1], more, 0)
        done = acc[...].astype(BF16).reshape(8, NCH, 16, BS)
        for j in range(NCH):
            out_ref[j, r] = done[:, j].reshape(MC, BS)
        return 0

    lax.fori_loop(0, NB, row, 0)


def mass_product(slot, colm, start, tmat, low, up, mass):
    smem = pl.BlockSpec(memory_space=pltpu.SMEM)
    vmem = pl.BlockSpec(memory_space=pltpu.VMEM)
    return pl.pallas_call(
        product_kernel,
        out_shape=jax.ShapeDtypeStruct((NCH, NB, MC, BS), BF16),
        in_specs=[smem] * 3 + [vmem] * 4,
        out_specs=vmem,
        scratch_shapes=[pltpu.VMEM((NB + 4, W, BS), BF16), pltpu.VMEM((W, BS), F32)],
        compiler_params=pltpu.CompilerParams(vmem_limit_bytes=48 << 20),
        name="mass_product",
    )(slot, colm, start, tmat, low, up, mass)


def couple_kernel(
    x_ref, tmat_hbm, out_ref, buf, tmat, accs, pairbuf, parts,
    load_sem, recv_sem, send_sem, pair_send, pair_recv, part_send, part_recv,
):
    col = lax.axis_index("col")
    dom = lax.axis_index("dom")
    core, zed, yhi = dom % 2, dom // 2 % 8, dom // 16
    chip = yhi * 8 + zed
    sibling = dom + 1 - 2 * core
    root = col == 7
    tables = tree_tables()
    depths = [pick(t[0], col) for t in tables]
    kids = [[pick(t[1], col), pick(t[2], col)] for t in tables]

    barrier = pltpu.get_barrier_semaphore()
    xpos, ylo = col // 2, col % 2
    for near in ((xpos + 1) % 4 * 2 + ylo, (xpos + 3) % 4 * 2 + ylo, xpos * 2 + 1 - ylo):
        pl.semaphore_signal(barrier, inc=1, device_id={"col": near})
    pl.semaphore_signal(barrier, inc=1, device_id={"dom": sibling})
    for step in range(1, 16):
        far = (chip + step) % 16
        pl.semaphore_signal(barrier, inc=1, device_id={"dom": far * 2 + core})
    tmat_load = pltpu.make_async_copy(tmat_hbm, tmat, load_sem.at[NCH])
    tmat_load.start()

    def own_load(j):
        return pltpu.make_async_copy(x_ref.at[j], buf.at[j], load_sem.at[j])

    @pl.when(root)
    def _():
        for j in range(NCH):
            own_load(j).start()

    pl.semaphore_wait(barrier, 19)

    def piece(t, s, j, b):
        return pltpu.make_async_remote_copy(
            src_ref=buf.at[j, b], dst_ref=buf.at[j, b],
            send_sem=send_sem.at[t, s], recv_sem=recv_sem.at[j, b],
            device_id={"col": kids[t][s]},
        )

    def contract(j, i):
        lhs = jnp.concatenate([buf[j, 4 * i + u] for u in range(4)], axis=1)
        rhs = tmat[pl.ds(pl.multiple_of(i * 512, 512), 512), :]
        accs[j] += jnp.dot(lhs, rhs, preferred_element_type=F32)

    def pair_copy(j):
        return pltpu.make_async_remote_copy(
            src_ref=accs.at[j], dst_ref=pairbuf.at[j // 2],
            send_sem=pair_send.at[j // 2], recv_sem=pair_recv.at[j // 2],
            device_id={"dom": sibling},
        )

    def part_copy(j, q):
        target = q // 4 * 16 + (q % 4 * 2 + j // 2) * 2 + core
        return target, pltpu.make_async_remote_copy(
            src_ref=accs.at[j, pl.ds(q * 16, 16)], dst_ref=parts.at[chip],
            send_sem=part_send.at[j // 2, q], recv_sem=part_recv.at[chip],
            device_id={"dom": target},
        )

    def hand_over(j):
        @pl.when(core != j % 2)
        def _():
            pair_copy(j).start()

    def spread(j):
        @pl.when(core == j % 2)
        def _():
            pair_copy(j).wait_recv()
            accs[j] += pairbuf[j // 2]
            for q in range(8):
                target, copy = part_copy(j, q)

                @pl.when(target != dom)
                def _():
                    copy.start()

                @pl.when(target == dom)
                def _():
                    parts[chip] = accs[j, q * 16:(q + 1) * 16]

    accs[...] = jnp.zeros_like(accs)

    def tick(k, _):
        @pl.when(root & (k < NCH * PER) & (k % PER == 0))
        def _():
            own_load(k // PER).wait()

        for t in range(3):
            p = k - OFF * depths[t]
            j, i = p // PER, p % PER
            b = FIRST[t] + i

            @pl.when((p >= 0) & (p < NCH * PER) & (i < FIRST[t + 1] - FIRST[t]))
            def _():
                @pl.when(depths[t] > 0)
                def _():
                    piece(t, 0, j, b).wait_recv()

                for s in range(2):
                    @pl.when(kids[t][s] >= 0)
                    def _():
                        piece(t, s, j, b).start()

        m = k - (PER + 4 * OFF)

        @pl.when(m == 0)
        def _():
            tmat_load.wait()

        @pl.when(m >= 0)
        def _():
            j, i = m // PER, m % PER

            @pl.when(i < 8)
            def _():
                contract(j, i)

            @pl.when(i == 8)
            def _():
                hand_over(j)

            @pl.when(i == 10)
            def _():
                spread(j)

        return 0

    lax.fori_loop(0, NCH * PER + 4 * OFF, tick, 0)
    last = NCH - 1
    lax.fori_loop(0, 8, lambda i, _: (contract(last, i), 0)[1], 0)
    hand_over(last)
    spread(last)

    for t in range(3):
        for s in range(2):
            @pl.when(kids[t][s] >= 0)
            def _():
                region = buf.at[:, pl.ds(FIRST[t], FIRST[t + 1] - FIRST[t])]
                pltpu.make_async_remote_copy(
                    src_ref=region, dst_ref=region, send_sem=send_sem.at[t, s],
                    recv_sem=recv_sem.at[0, 0], device_id={"col": kids[t][s]},
                ).wait_send()
    for j in range(NCH):
        @pl.when(core != j % 2)
        def _():
            pair_copy(j).wait_send()

        @pl.when(core == j % 2)
        def _():
            for q in range(8):
                target, copy = part_copy(j, q)

                @pl.when(target != dom)
                def _():
                    copy.wait_send()

    for step in range(1, 16):
        source = (chip + step) % 16
        pltpu.make_async_remote_copy(
            src_ref=parts.at[0], dst_ref=parts.at[source],
            send_sem=part_send.at[0, 0], recv_sem=part_recv.at[source],
            device_id={"dom": source * 2 + core},
        ).wait_recv()
    total = parts[0]
    for s in range(1, 16):
        total = total + parts[s]
    out_ref[...] = total


def couple(x, tmat):
    anyspace = pl.BlockSpec(memory_space=pl.ANY)
    return pl.pallas_call(
        couple_kernel,
        out_shape=jax.ShapeDtypeStruct((16, W), F32),
        in_specs=[anyspace, anyspace],
        out_specs=pl.BlockSpec(memory_space=pltpu.VMEM),
        scratch_shapes=[
            pltpu.VMEM((NCH, NB, MC, BS), BF16),
            pltpu.VMEM((NB * BS, W), BF16),
            pltpu.VMEM((NCH, MC, W), F32),
            pltpu.VMEM((2, MC, W), F32),
            pltpu.VMEM((16, 16, W), F32),
            pltpu.SemaphoreType.DMA((NCH + 1,)),
            pltpu.SemaphoreType.DMA((NCH, NB)),
            pltpu.SemaphoreType.DMA((3, 2)),
            pltpu.SemaphoreType.DMA((2,)),
            pltpu.SemaphoreType.DMA((2,)),
            pltpu.SemaphoreType.DMA((2, 8)),
            pltpu.SemaphoreType.DMA((16,)),
        ],
        compiler_params=pltpu.CompilerParams(
            collective_id=0, has_side_effects=True, vmem_limit_bytes=32 << 20
        ),
        name="couple",
    )(x, tmat)


def passed_along(block, axis, distance):
    devices = range(lax.axis_size(axis))
    route = [(i - distance, i) for i in devices if i - distance in devices]
    return lax.ppermute(block, axis, route)


def plan(block_index, live_block_count):
    slots = jnp.arange(NS, dtype=jnp.int32)
    key = jnp.where(slots < live_block_count[0], block_index[:, 0], NB)
    rows = jnp.arange(NB, dtype=jnp.int32)
    pairs = (jnp.sum((key[None, :] == rows[:, None]).astype(jnp.int32), axis=1) + 1) // 2
    edges = jnp.arange(NB + 1, dtype=jnp.int32)
    start = jnp.sum(jnp.where(rows[None, :] < edges[:, None], pairs[None, :], 0), axis=1)
    before = jnp.sum(((key[None, :] == key[:, None]) & (slots[None, :] < slots[:, None])).astype(jnp.int32), axis=1)
    base = jnp.sum(jnp.where(key[:, None] == edges[None, :], start[None, :], 0), axis=1)
    place = jnp.where(key < NB, 2 * base + before, 2 * NPAIR)
    hit = jnp.arange(2 * NPAIR, dtype=jnp.int32)[:, None] == place[None, :]
    slot = NS - jnp.sum(jnp.where(hit, NS - slots[None, :], 0), axis=1)
    colm = jnp.sum(jnp.where(hit, block_index[None, :, 1], 0), axis=1)
    return slot.astype(jnp.int32), colm.astype(jnp.int32), start.astype(jnp.int32)


def body(tmat, stored_mass_blocks, block_index, live_block_count, send_rows):
    slot, colm, start = plan(block_index, live_block_count)
    from_lower = passed_along(jnp.take(tmat, send_rows[1], axis=0), "dom", 1)
    from_upper = passed_along(jnp.take(tmat, send_rows[0], axis=0), "dom", -1)
    mass = jnp.concatenate([stored_mass_blocks, jnp.zeros((1, BS, BS), BF16)], 0)
    x = mass_product(slot, colm, start, tmat, from_lower, from_upper, mass)
    return couple(x, tmat)


def solution(mesh):
    return jax.shard_map(
        body,
        mesh=mesh,
        in_specs=(P("dom", "col"), P("dom", None, None), P("dom", None), P("dom"), P("dom", None)),
        out_specs=P("dom", "col"),
        check_vma=False,
    )
```

time: 750 us -> 147 us (0.20)
  waiting for transfers between devices: 462 us -> 0.01 us
  other arithmetic: 158 us -> 0.95 us
  Pallas kernels: 0 us -> 120 us
  matrix products: 52 us -> 0 us
  local copies, waits for them, and re-layouts: 48.4 us -> 19.6 us
  between operations: 14.2 us -> 0.8 us
    psum x2 -> x0, waiting for transfers between devices: 457 us -> none  [the longest x1 266 us: body(): total = lax.psum(contract(interface_mass_panel, tmat), 'dom')]
    scatter-add x4 -> x0, other arithmetic: 147 us -> none  [step(): acc = acc.at[targets].add(prod * weights[:, None, None])]
    pallas_call x0 -> x2, Pallas kernels: none -> 120 us  [the longest x1 94.8 us: couple(): pl.pallas_call(couple_kernel, out_shape=jax.ShapeDtypeStruct((16, W), F32...]
    dot_general x5 -> x0, matrix products: 52 us -> none  [the longest x4 48.6 us: step(): jnp.einsum('kab,kbw->kaw', blocks, selected, preferred_element_type=jnp.f...]
    gather x6 -> x2, local copies, waits for them, and re-layouts: 39.3 us -> 7.88 us  [the longest x1 3.94 us: body(): from_upper = passed_along(jnp.take(tmat, send_rows[0], axis=0), 'dom', -1)]
    concatenate x0 -> x1, local copies, waits for them, and re-layouts: none -> 10.3 us  [body(): jnp.concatenate([stored_mass_blocks, jnp.zeros((1, BS, BS), BF16)], 0)]
  transfers between devices with their start and end apart: 4 -> 2, of which waited for: 3 -> 0; matrix products, arithmetic and copies ran while one was open for 1% -> 10% of each run, Pallas kernels for 0% -> 0%
where the time goes in v1:
time: 147 us
  Pallas kernels  120 us (82%)
  local copies, waits for them, and re-layouts  19.6 us (13%)
  starting transfers between devices  6.03 us (4%)
    pallas_call x1, Pallas kernels, couple(): pl.pallas_call(couple_kernel, out_shape=jax.ShapeDtypeStruct((16, W), F32...  94.8 us
    pallas_call x1, Pallas kernels, mass_product(): pl.pallas_call(product_kernel, out_shape=jax.ShapeDtypeStruct((NCH, NB, M...  25 us
    concatenate x1, local copies, waits for them, and re-layouts, body(): jnp.concatenate([stored_mass_blocks, jnp.zeros((1, BS, BS), BF16)], 0)  10.3 us
    ppermute x2, starting transfers between devices, passed_along(): return lax.ppermute(block, axis, route)  6.03 us
    gather x1, local copies, waits for them, and re-layouts, body(): from_upper = passed_along(jnp.take(tmat, send_rows[0], axis=0), 'dom', -1)  3.94 us
    gather x1, local copies, waits for them, and re-layouts, body(): from_lower = passed_along(jnp.take(tmat, send_rows[1], axis=0), 'dom', 1)  3.94 us
  transfers between devices with their start and end apart: 2, of which 0 were waited for; matrix products, arithmetic and copies ran while one was open for 10% of the time, Pallas kernels for 0%

profile of v1, /device:TPU:33, one launch (start us, length us, event | category | flops | bytes accessed | tf_op | source)
XLA Modules:
  0.0 147.2 jit_solution(10090425051204531186)
XLA Ops:
  0.0 0.0 copy-start.1
  0.0 0.8 fusion.1
  0.8 3.9 %gather_fusion.1 = bf16[256,512]{1,0:T(8,128)(2,1)S(1)} fusion(bf16[4096,512]{1,0:T(8,128)(2,1)} %tmat_hbm.1, s32[1024]{0:T(1024)S(1)} %pad_clamp_fusion), kind=kCustom, calls=%fused_computation.1.clone | custom fusion | bytes 525312 | tf_op jit(solution)/shard_map/jit(_take)/gather | solution.py:339
  4.7 0.1 broadcast_select_fusion
  4.9 2.6 %collective-permute-start.1 = (bf16[256,512]{1,0:T(8,128)(2,1)S(1)}, bf16[256,512]{1,0:T(8,128)(2,1)S(1)}, u32[]{:S(2)}, u32[]{:S(2)}) collective-permute-start(bf16[256,512]{1,0:T(8,128)(2,1)S(1)} %broadcast_select_fusion), channel_id=1, source_target_pairs={{8,0},{16,8},{24,16},{32,24},{40,32},{48,40},{56,48},{64,56},{72,6... | collective-permute-start | bytes 786440 | tf_op jit(solution)/shard_map/ppermute | solution.py:317
  7.5 3.9 %gather_fusion = bf16[256,512]{1,0:T(8,128)(2,1)S(1)} fusion(bf16[4096,512]{1,0:T(8,128)(2,1)} %tmat_hbm.1, s32[1024]{0:T(1024)S(1)} %pad_clamp_fusion.1), kind=kCustom, calls=%fused_computation.clone | custom fusion | bytes 525312 | tf_op jit(solution)/shard_map/jit(_take)/gather | solution.py:338
  11.4 0.1 broadcast_select_fusion.1
  11.5 3.4 %collective-permute-start = (bf16[256,512]{1,0:T(8,128)(2,1)S(1)}, bf16[256,512]{1,0:T(8,128)(2,1)S(1)}, u32[]{:S(2)}, u32[]{:S(2)}) collective-permute-start(bf16[256,512]{1,0:T(8,128)(2,1)S(1)} %broadcast_select_fusion.1), channel_id=1, source_target_pairs={{0,8},{8,16},{16,24},{24,32},{32,40},{40,48},{48,56},{56,64},{64,7... | collective-permute-start | bytes 786440 | tf_op jit(solution)/shard_map/ppermute | solution.py:317
  15.6 0.0 copy-done.1
  15.7 0.1 convert_reduce_fusion.1
  15.8 0.2 convert_reduce_fusion
  16.0 0.1 select_reduce_fusion.3.start_ref
  16.1 0.1 select_reduce_fusion.2
  16.2 0.2 select_reduce_fusion
  16.4 10.3 %concatenate.3.mass_ref = bf16[257,128,128]{2,1,0:T(8,128)(2,1)} pad(bf16[256,128,128]{2,1,0:T(8,128)(2,1)} %param.8, bf16[]{:T(256)} %constant.37.clone.1), padding=0_1x0_0x0_0 | pad | bytes 16809986 | tf_op jit(solution)/shard_map/concatenate | solution.py:340
  26.7 0.0 collective-permute-done.1.up_ref
  26.7 0.0 collective-permute-done.low_ref
  26.7 0.0 copy-start
  26.7 25.0 %mass_product.1.x_ref = bf16[4,32,128,128]{3,2,1,0:T(8,128)(2,1)S(1)} custom-call(s32[288]{0:T(512)S(1)} %broadcast_subtract_fusion.slot_ref, s32[288]{0:T(512)S(1)} %get-tuple-element.6.colm_ref, s32[33]{0:T(128)S(1)} %select_reduce_fusion.3.start_ref, bf16[4096,512]{1,0:T(8,128)(2,1)} %tmat_hbm.1, bf16[256,512]{1,0:T(8,128)(2,1)S(1)} %collective-permute-done.low_ref, ...), custom_call_target="tpu_custom_call" | custom-call | tf_op jit(solution)/shard_map/mass_product/pallas_call | solution.py:103
  51.8 0.0 copy-done
  51.8 94.8 %couple.1 = f32[16,512]{1,0:T(8,128)S(1)} custom-call(bf16[4,32,128,128]{3,2,1,0:T(8,128)(2,1)S(1)} %mass_product.1.x_ref, bf16[4096,512]{1,0:T(8,128)(2,1)S(1)} %copy-done), custom_call_target="tpu_custom_call" | custom-call | tf_op jit(solution)/shard_map/couple/pallas_call | solution.py:288
  146.6 0.6 copy.8
  (11 shorter events, 0.1 us)
Async XLA Ops:
  0.0 15.6 %copy-start.1 = (s32[256,2]{0,1:T(2,128)S(1)}, s32[256,2]{0,1:T(2,128)}, u32[]{:S(2)}) copy-start(s32[256,2]{0,1:T(2,128)} %param.9) | copy-start | bytes 6148
  4.9 21.9 %collective-permute-start.1 = (bf16[256,512]{1,0:T(8,128)(2,1)S(1)}, bf16[256,512]{1,0:T(8,128)(2,1)S(1)}, u32[]{:S(2)}, u32[]{:S(2)}) collective-permute-start(bf16[256,512]{1,0:T(8,128)(2,1)S(1)} %broadcast_select_fusion), channel_id=1, source_target_pairs={{8,0},{16,8},{24,16},{32,24},{40,32},{48,40},{56,48},{64,56},{72,6... | collective-permute-start | bytes 786440 | tf_op jit(solution)/shard_map/ppermute | solution.py:317
  11.5 15.2 %collective-permute-start = (bf16[256,512]{1,0:T(8,128)(2,1)S(1)}, bf16[256,512]{1,0:T(8,128)(2,1)S(1)}, u32[]{:S(2)}, u32[]{:S(2)}) collective-permute-start(bf16[256,512]{1,0:T(8,128)(2,1)S(1)} %broadcast_select_fusion.1), channel_id=1, source_target_pairs={{0,8},{8,16},{16,24},{24,32},{32,40},{40,48},{48,56},{56,64},{64,7... | collective-permute-start | bytes 786440 | tf_op jit(solution)/shard_map/ppermute | solution.py:317
  26.7 25.1 %copy-start = (bf16[4096,512]{1,0:T(8,128)(2,1)S(1)}, bf16[4096,512]{1,0:T(8,128)(2,1)}, u32[]{:S(2)}) copy-start(bf16[4096,512]{1,0:T(8,128)(2,1)} %tmat_hbm.1) | copy-start | bytes 12582916

commit v2 on v1

v2 whole, which is shorter than its diff:
```python
import functools

import jax
import jax.numpy as jnp
from jax import lax
from jax.experimental import pallas as pl
from jax.experimental.pallas import tpu as pltpu
from jax.sharding import PartitionSpec as P

F32 = jnp.float32
BF16 = jnp.bfloat16
BS = 128
W = 512
NB = 32
NS = 256
NPAIR = (NS + NB) // 2
NCH = 4
MC = W // NCH
OFF = 6
PER = 11
RAW = 2
HALF = 256
UNR = 8

TREES = (
    ("00>10", "10>20", "20>21", "21>31", "10>11", "11>01", "20>30"),
    ("00>30", "30>20", "20>10", "30>31", "31>21", "21>11", "31>01"),
    ("00>01", "01>11", "11>21", "21>20", "01>31", "31>30", "11>10"),
)
FIRST = (0, 11, 22, 32)
HALO = (0, 3, 6, 8)
T_HALO = RAW * PER
T_MASS = T_HALO + 3
T_END = T_MASS + (NCH - RAW) * PER


def column_of(node):
    x, y = int(node[0]), int(node[1])
    return (x + 3) % 4 * 2 + 1 - y


def tree_tables():
    tables = []
    for edges in TREES:
        kids = [[-1, -1] for _ in range(8)]
        depth = [0] * 8
        for edge in edges:
            a, b = (column_of(n) for n in edge.split(">"))
            depth[b] = depth[a] + 1
            kids[a][0 if kids[a][0] < 0 else 1] = b
        tables.append((depth, [k[0] for k in kids], [k[1] for k in kids]))
    return tables


def pick(values, index):
    out = jnp.int32(values[0])
    for i, v in enumerate(values[1:], 1):
        out = jnp.where(index == i, jnp.int32(v), out)
    return out


def couple_kernel(
    slot_ref, colm_ref, keep_ref, last_ref, idx_ref, tmat_hbm, mass_hbm, out_ref,
    ext, xt, steps, acc, tmat, mass, perm, eye, lists, accs, pairbuf, parts,
    load_sem, halo_send, halo_recv, raw_recv, x_recv, send_sem,
    pair_send, pair_recv, part_send, part_recv,
):
    col = lax.axis_index("col")
    dom = lax.axis_index("dom")
    core, zed, yhi = dom % 2, dom // 2 % 8, dom // 16
    chip = yhi * 8 + zed
    sibling = dom + 1 - 2 * core
    root = col == 7
    tables = tree_tables()
    depths = [pick(t[0], col) for t in tables]
    kids = [[pick(t[1], col), pick(t[2], col)] for t in tables]

    def loop(n, f):
        def step(i, _):
            f(i)
            return 0

        lax.fori_loop(0, n, step, 0)

    tmat_load = pltpu.make_async_copy(tmat_hbm, tmat, load_sem.at[0])
    tmat_load.start()
    mass_load = pltpu.make_async_copy(mass_hbm, mass.at[pl.ds(0, NS)], load_sem.at[1])
    mass_load.start()

    barrier = pltpu.get_barrier_semaphore()
    xpos, ylo = col // 2, col % 2
    for near in ((xpos + 1) % 4 * 2 + ylo, (xpos + 3) % 4 * 2 + ylo, xpos * 2 + 1 - ylo):
        pl.semaphore_signal(barrier, inc=1, device_id={"col": near})
    for near in ((dom + 1) % 32, (dom + 31) % 32):
        pl.semaphore_signal(barrier, inc=1, device_id={"dom": near})

    def greet(step):
        far = (chip + step + 1) % 16
        pl.semaphore_signal(barrier, inc=1, device_id={"dom": far * 2 + core})

    loop(15, greet)

    mass[NS] = jnp.zeros((BS, BS), BF16)
    eye[...] = (
        lax.broadcasted_iota(jnp.int32, (HALF, HALF), 0) == lax.broadcasted_iota(jnp.int32, (HALF, HALF), 1)
    ).astype(BF16)

    def piece(kind, t, j, b, target, s):
        ref = ext.at[j, b] if kind < 2 else xt.at[RAW + j, b]
        sem = raw_recv.at[j, b] if kind < 2 else x_recv.at[j, b]
        return pltpu.make_async_remote_copy(
            src_ref=ref, dst_ref=ref, send_sem=send_sem.at[t, s, kind], recv_sem=sem,
            device_id={"col": target},
        )

    def mass_step(half, k):
        prods = []
        for u in range(UNR):
            q = k * UNR + u
            c1, c2 = colm_ref[2 * q], colm_ref[2 * q + 1]
            blocks = jnp.concatenate([mass[slot_ref[2 * q]], mass[slot_ref[2 * q + 1]]], axis=1)
            rows = jnp.concatenate(
                [jnp.concatenate([ext[2 * half, c], ext[2 * half + 1, c]], axis=1) for c in (c1, c2)], axis=0
            )
            prods.append(jnp.dot(blocks, rows, preferred_element_type=F32))
        total = acc[...]
        for u in range(UNR):
            total = total * keep_ref[k * UNR + u] + prods[u]
            steps[k * UNR + u] = total.astype(BF16)
        acc[...] = total

    def turn(half, r):
        done = lax.dot_general(
            eye[...], steps[last_ref[r]], (((1,), (1,)), ((), ())), preferred_element_type=F32
        ).astype(BF16)
        xt[2 * half, r] = done[:MC]
        xt[2 * half + 1, r] = done[MC:]

    def contract(j, i):
        lhs = jnp.concatenate([xt[j, 4 * i + u] for u in range(4)], axis=1)
        rhs = tmat[pl.ds(pl.multiple_of(i * 512, 512), 512), :]
        accs[j] += jnp.dot(lhs, rhs, preferred_element_type=F32)

    def pair_copy(j):
        return pltpu.make_async_remote_copy(
            src_ref=accs.at[j], dst_ref=pairbuf.at[j // 2],
            send_sem=pair_send.at[j // 2], recv_sem=pair_recv.at[j // 2],
            device_id={"dom": sibling},
        )

    def part_copy(j, q):
        target = q // 4 * 16 + (q % 4 * 2 + j // 2) * 2 + core
        return target, pltpu.make_async_remote_copy(
            src_ref=accs.at[j, pl.ds(pl.multiple_of(q * 16, 16), 16)], dst_ref=parts.at[chip],
            send_sem=part_send.at[j // 2, q], recv_sem=part_recv.at[chip],
            device_id={"dom": target},
        )

    def hand_over(j):
        @pl.when(core != j % 2)
        def _():
            pair_copy(j).start()

    def spread(j):
        @pl.when(core == j % 2)
        def _():
            pair_copy(j).wait_recv()
            accs[j] += pairbuf[j // 2]

            def send_part(q):
                target, copy = part_copy(j, q)

                @pl.when(target != dom)
                def _():
                    copy.start()

                @pl.when(target == dom)
                def _():
                    parts[chip] = accs[j, pl.ds(pl.multiple_of(q * 16, 16), 16)]

            loop(8, send_part)

    def from_root(kind, t, j, b):
        piece(kind, t, j, b, pick(tables[t][1], jnp.int32(7)), 0).start()

    @pl.when(root)
    def _():
        mode = lax.broadcasted_iota(jnp.int32, (W, W), 0)
        place = lax.broadcasted_iota(jnp.int32, (W, W), 1)
        wanted = (place // 16 % 8) * 64 + (place // MC) * 16 + place % 16
        perm[...] = (mode == wanted).astype(BF16)
        tmat_load.wait()
        pl.semaphore_wait(barrier, 20)

        def arrange(i):
            for t in range(3):
                b = FIRST[t] + i

                @pl.when(i < FIRST[t + 1] - FIRST[t])
                def _():
                    rows = tmat[pl.ds(pl.multiple_of(b * BS, BS), BS), :]
                    turned = jnp.dot(rows, perm[...], preferred_element_type=F32).astype(BF16)
                    for j in range(NCH):
                        ext[j, b] = turned[:, j * MC:(j + 1) * MC]
                    from_root(0, t, 0, b)

        loop(PER, arrange)

        def second(i):
            for t in range(3):
                @pl.when(i < FIRST[t + 1] - FIRST[t])
                def _():
                    from_root(0, t, 1, FIRST[t] + i)

        loop(PER, second)

        accs[...] = jnp.zeros_like(accs)

        def gather(k):
            lane = lax.broadcasted_iota(jnp.int32, (4 * BS, BS), 1)
            picks = jnp.concatenate(
                [(idx_ref[...] == lane + (k * 4 + u) * BS).astype(BF16) for u in range(4)], axis=1
            )
            rows = jnp.concatenate(
                [jnp.concatenate([ext[j, k * 4 + u] for j in range(NCH)], axis=1) for u in range(4)], axis=0
            )
            got = jnp.dot(picks, rows, preferred_element_type=F32)
            for h in range(4):
                accs[h] += got[h * BS:(h + 1) * BS]

        loop(NB // 4, gather)
        for h in range(4):
            got = accs[h].astype(BF16)
            for j in range(NCH):
                lists[j, h] = got[:, j * MC:(j + 1) * MC]

        def to_upper():
            return pltpu.make_async_remote_copy(
                src_ref=lists.at[:, pl.ds(2, 2)], dst_ref=ext.at[:, pl.ds(NB, 2)],
                send_sem=halo_send.at[0], recv_sem=halo_recv.at[0], device_id={"dom": (dom + 1) % 32},
            )

        def to_lower():
            return pltpu.make_async_remote_copy(
                src_ref=lists.at[:, pl.ds(0, 2)], dst_ref=ext.at[:, pl.ds(NB + 2, 2)],
                send_sem=halo_send.at[1], recv_sem=halo_recv.at[1], device_id={"dom": (dom + 31) % 32},
            )

        @pl.when(dom < 31)
        def _():
            to_upper().start()

        @pl.when(dom > 0)
        def _():
            to_lower().start()

        mass_load.wait()

        @pl.when(dom > 0)
        def _():
            to_upper().wait_recv()

        @pl.when(dom == 0)
        def _():
            ext[:, NB:NB + 2] = jnp.zeros((NCH, 2, BS, MC), BF16)

        @pl.when(dom < 31)
        def _():
            to_lower().wait_recv()

        @pl.when(dom == 31)
        def _():
            ext[:, NB + 2:NB + 4] = jnp.zeros((NCH, 2, BS, MC), BF16)

        for t in range(3):
            for h in range(HALO[t], HALO[t + 1]):
                from_root(1, t, h // 4, NB + h % 4)

        def half_product(turn_number):
            half = 1 - turn_number
            acc[...] = jnp.zeros_like(acc)
            loop(NPAIR // UNR, functools.partial(mass_step, half))

            def turn_send(i):
                for t in range(3):
                    @pl.when(i < FIRST[t + 1] - FIRST[t])
                    def _():
                        turn(half, FIRST[t] + i)

                        @pl.when(half == 1)
                        def _():
                            from_root(2, t, 0, FIRST[t] + i)

            loop(PER, turn_send)

            @pl.when(half == 1)
            def _():
                def send_last(i):
                    for t in range(3):
                        @pl.when(i < FIRST[t + 1] - FIRST[t])
                        def _():
                            from_root(2, t, 1, FIRST[t] + i)

                loop(PER, send_last)

        loop(2, half_product)
        accs[...] = jnp.zeros_like(accs)

        def reduce_chunk(j):
            loop(8, functools.partial(contract, j))
            hand_over(j)

            @pl.when(j > 0)
            def _():
                spread(j - 1)

        loop(NCH - 1, reduce_chunk)
        spread(NCH - 2)

        @pl.when(dom < 31)
        def _():
            to_upper().wait_send()

        @pl.when(dom > 0)
        def _():
            to_lower().wait_send()

    def relay(kind, t, j, b):
        piece(kind, t, j, b, kids[t][0], 0).wait_recv()
        for s in range(2):
            @pl.when(kids[t][s] >= 0)
            def _():
                piece(kind, t, j, b, kids[t][s], s).start()

    @pl.when(jnp.logical_not(root))
    def _():
        accs[...] = jnp.zeros_like(accs)
        acc[...] = jnp.zeros_like(acc)
        pl.semaphore_wait(barrier, 20)

        def tick(k):
            for t in range(3):
                p = k - OFF * depths[t]
                count = FIRST[t + 1] - FIRST[t]

                @pl.when((p >= 0) & (p < T_HALO) & (p % PER < count))
                def _():
                    relay(0, t, p // PER, FIRST[t] + p % PER)

                h = HALO[t] + p - T_HALO

                @pl.when((p >= T_HALO) & (h < HALO[t + 1]))
                def _():
                    relay(1, t, h // 4, NB + h % 4)

                x = p - T_MASS

                @pl.when((x >= 0) & (p < T_END) & (x % PER < count))
                def _():
                    relay(2, t, x // PER, FIRST[t] + x % PER)

            m = k - (T_MASS + 4 * OFF)

            @pl.when(m == 0)
            def _():
                tmat_load.wait()
                mass_load.wait()

            @pl.when((m >= 0) & (m < 9))
            def _():
                loop(2, lambda u: mass_step(0, 2 * m + u))

            @pl.when((m >= 9) & (m < 13))
            def _():
                i = m - 9
                for u in range(8):
                    turn(0, i * 8 + u)
                loop(4, lambda u: contract(u // 2, 2 * i + u % 2))

            @pl.when(m == 13)
            def _():
                hand_over(0)
                hand_over(1)

            @pl.when((m >= 14) & (m < 18))
            def _():
                loop(2, lambda u: contract(2, 2 * (m - 14) + u))

            @pl.when(m == 16)
            def _():
                loop(RAW, spread)

            @pl.when(m == 18)
            def _():
                hand_over(2)

            @pl.when(m == 21)
            def _():
                spread(2)

        loop(T_END + 4 * OFF, tick)

    last = NCH - 1
    loop(8, functools.partial(contract, last))
    hand_over(last)
    spread(last)

    for t in range(3):
        for s in range(2):
            @pl.when(kids[t][s] >= 0)
            def _():
                count = FIRST[t + 1] - FIRST[t]
                for kind, region in (
                    (0, ext.at[pl.ds(0, RAW), pl.ds(FIRST[t], count)]),
                    (1, ext.at[0, pl.ds(NB, HALO[t + 1] - HALO[t])]),
                    (2, xt.at[pl.ds(RAW, NCH - RAW), pl.ds(FIRST[t], count)]),
                ):
                    pltpu.make_async_remote_copy(
                        src_ref=region, dst_ref=region, send_sem=send_sem.at[t, s, kind],
                        recv_sem=raw_recv.at[0, 0], device_id={"col": kids[t][s]},
                    ).wait_send()
    def finish(j):
        @pl.when(core != j % 2)
        def _():
            pair_copy(j).wait_send()

        @pl.when(core == j % 2)
        def _():
            def sent(q):
                target, copy = part_copy(j, q)

                @pl.when(target != dom)
                def _():
                    copy.wait_send()

            loop(8, sent)

    loop(NCH, finish)

    def arrived(step):
        source = (chip + step + 1) % 16
        pltpu.make_async_remote_copy(
            src_ref=parts.at[0], dst_ref=parts.at[source],
            send_sem=part_send.at[0, 0], recv_sem=part_recv.at[source],
            device_id={"dom": source * 2 + core},
        ).wait_recv()

    loop(15, arrived)
    total = parts[0]
    for s in range(1, 16):
        total = total + parts[s]
    out_ref[...] = total


def couple(slot, colm, keep, last, idx, tmat, mass):
    smem = pl.BlockSpec(memory_space=pltpu.SMEM)
    vmem = pl.BlockSpec(memory_space=pltpu.VMEM)
    anyspace = pl.BlockSpec(memory_space=pl.ANY)
    dma = pltpu.SemaphoreType.DMA
    return pl.pallas_call(
        couple_kernel,
        out_shape=jax.ShapeDtypeStruct((16, W), F32),
        in_specs=[smem] * 4 + [vmem, anyspace, anyspace],
        out_specs=vmem,
        scratch_shapes=[
            pltpu.VMEM((NCH, NB + 4, BS, MC), BF16),
            pltpu.VMEM((NCH, NB, MC, BS), BF16),
            pltpu.VMEM((NPAIR, BS, HALF), BF16),
            pltpu.VMEM((BS, HALF), F32),
            pltpu.VMEM((NB * BS, W), BF16),
            pltpu.VMEM((NS + 1, BS, BS), BF16),
            pltpu.VMEM((W, W), BF16),
            pltpu.VMEM((HALF, HALF), BF16),
            pltpu.VMEM((NCH, 4, BS, MC), BF16),
            pltpu.VMEM((NCH, MC, W), F32),
            pltpu.VMEM((2, MC, W), F32),
            pltpu.VMEM((16, 16, W), F32),
            dma((2,)), dma((2,)), dma((2,)), dma((RAW, NB + 4)), dma((NCH - RAW, NB)), dma((3, 2, 3)),
            dma((2,)), dma((2,)), dma((2, 8)), dma((16,)),
        ],
        compiler_params=pltpu.CompilerParams(
            collective_id=0, has_side_effects=True, vmem_limit_bytes=60 << 20
        ),
        name="couple",
    )(slot, colm, keep, last, idx, tmat, mass)


def plan(block_index, live_block_count):
    slots = jnp.arange(NS, dtype=jnp.int32)
    key = jnp.where(slots < live_block_count[0], block_index[:, 0], NB)
    rows = jnp.arange(NB, dtype=jnp.int32)
    pairs = (jnp.sum((key[None, :] == rows[:, None]).astype(jnp.int32), axis=1) + 1) // 2
    edges = jnp.arange(NB + 1, dtype=jnp.int32)
    start = jnp.sum(jnp.where(rows[None, :] < edges[:, None], pairs[None, :], 0), axis=1)
    before = jnp.sum(((key[None, :] == key[:, None]) & (slots[None, :] < slots[:, None])).astype(jnp.int32), axis=1)
    base = jnp.sum(jnp.where(key[:, None] == edges[None, :], start[None, :], 0), axis=1)
    place = jnp.where(key < NB, 2 * base + before, 2 * NPAIR)
    hit = jnp.arange(2 * NPAIR, dtype=jnp.int32)[:, None] == place[None, :]
    slot = NS - jnp.sum(jnp.where(hit, NS - slots[None, :], 0), axis=1)
    colm = jnp.sum(jnp.where(hit, block_index[None, :, 1], 0), axis=1)
    opens = jnp.any(jnp.arange(NPAIR, dtype=jnp.int32)[:, None] == start[None, :NB], axis=1)
    keep = 1.0 - opens.astype(F32)
    last = start[1:] - 1
    return slot.astype(jnp.int32), colm.astype(jnp.int32), keep, last.astype(jnp.int32)


def body(tmat, stored_mass_blocks, block_index, live_block_count, send_rows):
    slot, colm, keep, last = plan(block_index, live_block_count)
    idx = jnp.broadcast_to(send_rows.reshape(4 * BS, 1), (4 * BS, BS))
    return couple(slot, colm, keep, last, idx, tmat, stored_mass_blocks)


def solution(mesh):
    return jax.shard_map(
        body,
        mesh=mesh,
        in_specs=(P("dom", "col"), P("dom", None, None), P("dom", None), P("dom"), P("dom", None)),
        out_specs=P("dom", "col"),
        check_vma=False,
    )
```

time: 147 us -> 92.8 us (0.63)
  Pallas kernels: 120 us -> 84 us
  local copies, waits for them, and re-layouts: 19.6 us -> 2.88 us
  starting transfers between devices: 6.03 us -> 0 us
  other arithmetic: 0.95 us -> 3.94 us
    pallas_call x1 -> x0, Pallas kernels: 25 us -> none  [mass_product(): pl.pallas_call(product_kernel, out_shape=jax.ShapeDtypeStruct((NCH, NB, M...]
    pallas_call x1, Pallas kernels: 94.8 us -> 84 us  [couple(): pl.pallas_call(couple_kernel, out_shape=jax.ShapeDtypeStruct((16, W), F32...]
    concatenate x1 -> x0, local copies, waits for them, and re-layouts: 10.3 us -> none  [body(): jnp.concatenate([stored_mass_blocks, jnp.zeros((1, BS, BS), BF16)], 0)]
    gather x2 -> x0, local copies, waits for them, and re-layouts: 7.88 us -> none  [the longest x1 3.94 us: body(): from_upper = passed_along(jnp.take(tmat, send_rows[0], axis=0), 'dom', -1)]
    ppermute x2 -> x0, starting transfers between devices: 6.03 us -> none  [passed_along(): return lax.ppermute(block, axis, route)]
  transfers between devices with their start and end apart: 2 -> 0, of which waited for: 0 -> 0; matrix products, arithmetic and copies ran while one was open for 10% -> 0% of each run, Pallas kernels for 0% -> 0%
where the time goes in v2:
time: 92.8 us; the launch traced here: 91.5 us
  Pallas kernels  84 us (91%)
  other arithmetic  3.94 us (4%)
  local copies, waits for them, and re-layouts  2.88 us (3%)
    pallas_call x1, Pallas kernels, couple(): pl.pallas_call(couple_kernel, out_shape=jax.ShapeDtypeStruct((16, W), F32...  84 us
    unnamed x2, local copies, waits for them, and re-layouts  2.06 us

profile of v2, /device:TPU:33, one launch (start us, length us, event | category | flops | bytes accessed | tf_op | source)
XLA Modules:
  0.0 91.5 jit_solution(2948848763856124046)
XLA Ops:
  0.7 0.7 copy.6
  1.3 0.8 compare_select_fusion
  2.1 0.1 convert_reduce_fusion.1
  2.2 0.2 convert_reduce_fusion
  2.4 0.1 select_reduce_fusion.3
  2.5 0.1 select_reduce_fusion.2
  2.6 0.7 slice_add_fusion
  3.3 0.1 fusion.1
  3.4 0.6 convert_subtract_fusion.keep_ref
  4.0 0.7 select_reduce_fusion
  4.7 0.6 broadcast_subtract_fusion.slot_ref
  5.3 0.8 broadcast_in_dim.89.idx_ref
  6.1 84.0 %couple.1 = f32[16,512]{1,0:T(8,128)} custom-call(s32[288]{0:T(512)} %broadcast_subtract_fusion.slot_ref, s32[288]{0:T(512)} %get-tuple-element.5.colm_ref, f32[144]{0:T(256)} %convert_subtract_fusion.keep_ref, s32[32]{0:T(128)} %get-tuple-element.10.last_ref, s32[512,128]{1,0:T(8,128)} %broadcast_in_dim.89.idx_ref, bf16[4096,512]{1,0:T(8,128)(2,1)} %tmat_hbm.1, ...), custom_call_target="tpu_custom_call" | custom-call | tf_op jit(solution)/shard_map/couple/pallas_call | solution.py:460
  90.2 1.4 %copy.9 = f32[16,512]{1,0:T(8,128)} copy(f32[16,512]{1,0:T(8,128)} %couple.1) | data formatting | bytes 65536
  (3 shorter events, 0.0 us)

commit v3 on v2

--- a/solution.py
+++ b/solution.py
@@ -16,11 +16,11 @@
 NPAIR = (NS + NB) // 2
 NCH = 4
 MC = W // NCH
-OFF = 6
+OFF = 5
 PER = 11
-RAW = 2
+RAW = 1
 HALF = 256
-UNR = 8
+LIST = 384
 
 TREES = (
     ("00>10", "10>20", "20>21", "21>31", "10>11", "11>01", "20>30"),
@@ -28,9 +28,9 @@
     ("00>01", "01>11", "11>21", "21>20", "01>31", "31>30", "11>10"),
 )
 FIRST = (0, 11, 22, 32)
-HALO = (0, 3, 6, 8)
+HALO = (0, 2, 3, 4)
 T_HALO = RAW * PER
-T_MASS = T_HALO + 3
+T_MASS = T_HALO + 2
 T_END = T_MASS + (NCH - RAW) * PER
 
 
@@ -60,8 +60,8 @@
 
 
 def couple_kernel(
-    slot_ref, colm_ref, keep_ref, last_ref, idx_ref, tmat_hbm, mass_hbm, out_ref,
-    ext, xt, steps, acc, tmat, mass, perm, eye, lists, accs, pairbuf, parts,
+    live_ref, index_ref, shared_ref, tmat_hbm, mass_hbm, out_ref,
+    order_v, order, ext, xt, steps, acc, tmat, mass, perm, eye, lists, accs, pairbuf, parts,
     load_sem, halo_send, halo_recv, raw_recv, x_recv, send_sem,
     pair_send, pair_recv, part_send, part_recv,
 ):
@@ -85,7 +85,6 @@
     tmat_load = pltpu.make_async_copy(tmat_hbm, tmat, load_sem.at[0])
     tmat_load.start()
     mass_load = pltpu.make_async_copy(mass_hbm, mass.at[pl.ds(0, NS)], load_sem.at[1])
-    mass_load.start()
 
     barrier = pltpu.get_barrier_semaphore()
     xpos, ylo = col // 2, col % 2
@@ -113,28 +112,60 @@
             device_id={"col": target},
         )
 
-    def mass_step(half, k):
+    def plan():
+        I32 = jnp.int32
+
+        def iota(shape, axis):
+            return lax.broadcasted_iota(I32, shape, axis)
+
+        def add(condition, values, axis):
+            return jnp.sum(jnp.where(condition, values, 0), axis=axis, keepdims=True)
+
+        down = iota((NS, 1), 0)
+        key = jnp.where(down < live_ref[0], index_ref[:, 0:1], NB)
+        key_lane = add(iota((NS, NS), 0) == iota((NS, NS), 1), key, 0)
+        before = add((key == key_lane) & (iota((NS, NS), 1) < iota((NS, NS), 0)), 1, 1)
+        pairs_lane = (add(key == iota((NS, BS), 1), 1, 0) + 1) // 2
+        pairs = (add(iota((NB, NS), 0) == key_lane, 1, 1) + 1) // 2
+        base = add(iota((NS, BS), 1) < key, pairs_lane, 1)
+        start = add(iota((NB, BS), 1) < iota((NB, BS), 0), pairs_lane, 1)
+        place = jnp.where(key < NB, 2 * base + before, LIST)
+        hit = place == iota((NS, LIST), 1)
+        order_v[...] = jnp.zeros_like(order_v)
+        order_v[0:1] = jnp.clip(NS - add(hit, NS - down, 0), 0, NS)
+        order_v[1:2] = jnp.clip(add(hit, index_ref[:, 1:2], 0), 0, NB + 3)
+        order_v[2:3] = 1 - add(start == iota((NB, LIST), 1), 1, 0)
+        order_v[3:4] = jnp.clip(add(iota((NB, LIST), 0) <= iota((NB, LIST), 1), pairs, 0) - 1, 0, NPAIR - 1)
+        copy = pltpu.make_async_copy(order_v, order, load_sem.at[2])
+        copy.start()
+        copy.wait()
+
+    def mass_step(n, first, unr, k):
         prods = []
-        for u in range(UNR):
-            q = k * UNR + u
-            c1, c2 = colm_ref[2 * q], colm_ref[2 * q + 1]
-            blocks = jnp.concatenate([mass[slot_ref[2 * q]], mass[slot_ref[2 * q + 1]]], axis=1)
+        for u in range(unr):
+            q = k * unr + u
+            blocks = jnp.concatenate([mass[order[0, 2 * q]], mass[order[0, 2 * q + 1]]], axis=1)
             rows = jnp.concatenate(
-                [jnp.concatenate([ext[2 * half, c], ext[2 * half + 1, c]], axis=1) for c in (c1, c2)], axis=0
+                [
+                    jnp.concatenate([ext[first + v, order[1, 2 * q + w]] for v in range(n)], axis=1)
+                    for w in range(2)
+                ],
+                axis=0,
             )
             prods.append(jnp.dot(blocks, rows, preferred_element_type=F32))
-        total = acc[...]
-        for u in range(UNR):
-            total = total * keep_ref[k * UNR + u] + prods[u]
-            steps[k * UNR + u] = total.astype(BF16)
-        acc[...] = total
-
-    def turn(half, r):
+        total = acc[:, :n * MC]
+        for u in range(unr):
+            total = total * order[2, k * unr + u].astype(F32) + prods[u]
+            steps[k * unr + u, :, :n * MC] = total.astype(BF16)
+        acc[:, :n * MC] = total
+
+    def turn(n, first, r):
         done = lax.dot_general(
-            eye[...], steps[last_ref[r]], (((1,), (1,)), ((), ())), preferred_element_type=F32
+            eye[:n * MC, :n * MC], steps[order[3, r], :, :n * MC], (((1,), (1,)), ((), ())),
+            preferred_element_type=F32,
         ).astype(BF16)
-        xt[2 * half, r] = done[:MC]
-        xt[2 * half + 1, r] = done[MC:]
+        for v in range(n):
+            xt[first + v, r] = done[v * MC:(v + 1) * MC]
 
     def contract(j, i):
         lhs = jnp.concatenate([xt[j, 4 * i + u] for u in range(4)], axis=1)
@@ -189,51 +220,33 @@
         place = lax.broadcasted_iota(jnp.int32, (W, W), 1)
         wanted = (place // 16 % 8) * 64 + (place // MC) * 16 + place % 16
         perm[...] = (mode == wanted).astype(BF16)
+        plan()
         tmat_load.wait()
-        pl.semaphore_wait(barrier, 20)
-
-        def arrange(i):
-            for t in range(3):
-                b = FIRST[t] + i
-
-                @pl.when(i < FIRST[t + 1] - FIRST[t])
-                def _():
-                    rows = tmat[pl.ds(pl.multiple_of(b * BS, BS), BS), :]
-                    turned = jnp.dot(rows, perm[...], preferred_element_type=F32).astype(BF16)
-                    for j in range(NCH):
-                        ext[j, b] = turned[:, j * MC:(j + 1) * MC]
-                    from_root(0, t, 0, b)
-
-        loop(PER, arrange)
-
-        def second(i):
-            for t in range(3):
-                @pl.when(i < FIRST[t + 1] - FIRST[t])
-                def _():
-                    from_root(0, t, 1, FIRST[t] + i)
-
-        loop(PER, second)
-
+        mass_load.start()
+
+        square = (2 * BS, 2 * BS)
+        diagonal = lax.broadcasted_iota(jnp.int32, square, 0) == lax.broadcasted_iota(jnp.int32, square, 1)
+        wanted_rows = [
+            jnp.sum(jnp.where(diagonal, shared_ref[h:h + 1], 0), axis=1, keepdims=True) for h in range(2)
+        ]
+        idx = jnp.concatenate(wanted_rows, axis=0)
         accs[...] = jnp.zeros_like(accs)
 
         def gather(k):
-            lane = lax.broadcasted_iota(jnp.int32, (4 * BS, BS), 1)
-            picks = jnp.concatenate(
-                [(idx_ref[...] == lane + (k * 4 + u) * BS).astype(BF16) for u in range(4)], axis=1
-            )
-            rows = jnp.concatenate(
-                [jnp.concatenate([ext[j, k * 4 + u] for j in range(NCH)], axis=1) for u in range(4)], axis=0
-            )
+            lane = lax.broadcasted_iota(jnp.int32, (4 * BS, 8 * BS), 1)
+            picks = (idx == lane + k * 8 * BS).astype(BF16)
+            rows = tmat[pl.ds(pl.multiple_of(k * 8 * BS, 8 * BS), 8 * BS), :]
             got = jnp.dot(picks, rows, preferred_element_type=F32)
             for h in range(4):
                 accs[h] += got[h * BS:(h + 1) * BS]
 
-        loop(NB // 4, gather)
+        loop(NB // 8, gather)
         for h in range(4):
-            got = accs[h].astype(BF16)
+            got = jnp.dot(accs[h].astype(BF16), perm[...], preferred_element_type=F32).astype(BF16)
             for j in range(NCH):
                 lists[j, h] = got[:, j * MC:(j + 1) * MC]
 
+        pl.semaphore_wait(barrier, 20)
         def to_upper():
             return pltpu.make_async_remote_copy(
                 src_ref=lists.at[:, pl.ds(2, 2)], dst_ref=ext.at[:, pl.ds(NB, 2)],
@@ -254,6 +267,25 @@
         def _():
             to_lower().start()
 
+        def arrange(n, first, b):
+            rows = tmat[pl.ds(pl.multiple_of(b * BS, BS), BS), :]
+            turned = jnp.dot(rows, perm[:, first * MC:(first + n) * MC], preferred_element_type=F32).astype(BF16)
+            for v in range(n):
+                ext[first + v, b] = turned[:, v * MC:(v + 1) * MC]
+
+        def send_raw(i):
+            for t in range(3):
+                @pl.when(i < FIRST[t + 1] - FIRST[t])
+                def _():
+                    arrange(1, 0, FIRST[t] + i)
+                    from_root(0, t, 0, FIRST[t] + i)
+
+        def arrange_four(n, first, i):
+            for u in range(4):
+                arrange(n, first, 4 * i + u)
+
+        loop(PER, send_raw)
+        loop(NB // 4, functools.partial(arrange_four, 1, 1))
         mass_load.wait()
 
         @pl.when(dom > 0)
@@ -276,34 +308,26 @@
             for h in range(HALO[t], HALO[t + 1]):
                 from_root(1, t, h // 4, NB + h % 4)
 
-        def half_product(turn_number):
-            half = 1 - turn_number
+        def product(n, first, unr):
             acc[...] = jnp.zeros_like(acc)
-            loop(NPAIR // UNR, functools.partial(mass_step, half))
-
-            def turn_send(i):
-                for t in range(3):
-                    @pl.when(i < FIRST[t + 1] - FIRST[t])
-                    def _():
-                        turn(half, FIRST[t] + i)
-
-                        @pl.when(half == 1)
-                        def _():
-                            from_root(2, t, 0, FIRST[t] + i)
-
-            loop(PER, turn_send)
-
-            @pl.when(half == 1)
-            def _():
-                def send_last(i):
-                    for t in range(3):
-                        @pl.when(i < FIRST[t + 1] - FIRST[t])
-                        def _():
-                            from_root(2, t, 1, FIRST[t] + i)
-
-                loop(PER, send_last)
-
-        loop(2, half_product)
+            loop(NPAIR // unr, functools.partial(mass_step, n, first, unr))
+
+        def send_mass(n, first, j, i):
+            for t in range(3):
+                @pl.when(i < FIRST[t + 1] - FIRST[t])
+                def _():
+                    if n:
+                        turn(n, first, FIRST[t] + i)
+                    from_root(2, t, j, FIRST[t] + i)
+
+        product(1, 1, 16)
+        loop(PER, functools.partial(send_mass, 1, 1, 0))
+        loop(NB // 4, functools.partial(arrange_four, 2, 2))
+        product(2, 2, 8)
+        loop(PER, functools.partial(send_mass, 2, 2, 1))
+        loop(PER, functools.partial(send_mass, 0, 2, 2))
+        product(1, 0, 16)
+        loop(NB, functools.partial(turn, 1, 0))
         accs[...] = jnp.zeros_like(accs)
 
         def reduce_chunk(j):
@@ -336,6 +360,9 @@
     def _():
         accs[...] = jnp.zeros_like(accs)
         acc[...] = jnp.zeros_like(acc)
+        tmat_load.wait()
+        mass_load.start()
+        plan()
         pl.semaphore_wait(barrier, 20)
 
         def tick(k):
@@ -363,46 +390,46 @@
 
             @pl.when(m == 0)
             def _():
-                tmat_load.wait()
                 mass_load.wait()
 
-            @pl.when((m >= 0) & (m < 9))
-            def _():
-                loop(2, lambda u: mass_step(0, 2 * m + u))
-
-            @pl.when((m >= 9) & (m < 13))
-            def _():
-                i = m - 9
-                for u in range(8):
-                    turn(0, i * 8 + u)
-                loop(4, lambda u: contract(u // 2, 2 * i + u % 2))
-
-            @pl.when(m == 13)
-            def _():
-                hand_over(0)
-                hand_over(1)
-
-            @pl.when((m >= 14) & (m < 18))
-            def _():
-                loop(2, lambda u: contract(2, 2 * (m - 14) + u))
-
-            @pl.when(m == 16)
-            def _():
-                loop(RAW, spread)
-
-            @pl.when(m == 18)
-            def _():
-                hand_over(2)
-
-            @pl.when(m == 21)
-            def _():
-                spread(2)
+            @pl.when((m >= 0) & (m < 18))
+            def _():
+                mass_step(1, 0, 8, m)
+
+            @pl.when((m >= 12) & (m < 20))
+            def _():
+                contract(1, m - 12)
+
+            @pl.when((m >= 18) & (m < 26))
+            def _():
+                i = m - 18
+                for u in range(4):
+                    turn(1, 0, 4 * i + u)
+                contract(0, i)
+
+            @pl.when((m >= 23) & (m < 31))
+            def _():
+                contract(2, m - 23)
+
+            for j, at in ((1, 20), (0, 26), (2, 31)):
+                @pl.when(m == at)
+                def _():
+                    hand_over(j)
+
+            @pl.when((m == 24) | (m == 30))
+            def _():
+                spread((30 - m) // 6)
 
         loop(T_END + 4 * OFF, tick)
 
     last = NCH - 1
     loop(8, functools.partial(contract, last))
     hand_over(last)
+
+    @pl.when(jnp.logical_not(root))
+    def _():
+        spread(last - 1)
+
     spread(last)
 
     for t in range(3):
@@ -452,7 +479,7 @@
     out_ref[...] = total
 
 
-def couple(slot, colm, keep, last, idx, tmat, mass):
+def couple(live, index, shared, tmat, mass):
     smem = pl.BlockSpec(memory_space=pltpu.SMEM)
     vmem = pl.BlockSpec(memory_space=pltpu.VMEM)
     anyspace = pl.BlockSpec(memory_space=pl.ANY)
@@ -460,9 +487,11 @@
     return pl.pallas_call(
         couple_kernel,
         out_shape=jax.ShapeDtypeStruct((16, W), F32),
-        in_specs=[smem] * 4 + [vmem, anyspace, anyspace],
+        in_specs=[smem, vmem, vmem, anyspace, anyspace],
         out_specs=vmem,
         scratch_shapes=[
+            pltpu.VMEM((8, LIST), jnp.int32),
+            pltpu.SMEM((8, LIST), jnp.int32),
             pltpu.VMEM((NCH, NB + 4, BS, MC), BF16),
             pltpu.VMEM((NCH, NB, MC, BS), BF16),
             pltpu.VMEM((NPAIR, BS, HALF), BF16),
@@ -475,39 +504,18 @@
             pltpu.VMEM((NCH, MC, W), F32),
             pltpu.VMEM((2, MC, W), F32),
             pltpu.VMEM((16, 16, W), F32),
-            dma((2,)), dma((2,)), dma((2,)), dma((RAW, NB + 4)), dma((NCH - RAW, NB)), dma((3, 2, 3)),
+            dma((3,)), dma((2,)), dma((2,)), dma((RAW, NB + 4)), dma((NCH - RAW, NB)), dma((3, 2, 3)),
             dma((2,)), dma((2,)), dma((2, 8)), dma((16,)),
         ],
         compiler_params=pltpu.CompilerParams(
             collective_id=0, has_side_effects=True, vmem_limit_bytes=60 << 20
         ),
         name="couple",
-    )(slot, colm, keep, last, idx, tmat, mass)
-
-
-def plan(block_index, live_block_count):
-    slots = jnp.arange(NS, dtype=jnp.int32)
-    key = jnp.where(slots < live_block_count[0], block_index[:, 0], NB)
-    rows = jnp.arange(NB, dtype=jnp.int32)
-    pairs = (jnp.sum((key[None, :] == rows[:, None]).astype(jnp.int32), axis=1) + 1) // 2
-    edges = jnp.arange(NB + 1, dtype=jnp.int32)
-    start = jnp.sum(jnp.where(rows[None, :] < edges[:, None], pairs[None, :], 0), axis=1)
-    before = jnp.sum(((key[None, :] == key[:, None]) & (slots[None, :] < slots[:, None])).astype(jnp.int32), axis=1)
-    base = jnp.sum(jnp.where(key[:, None] == edges[None, :], start[None, :], 0), axis=1)
-    place = jnp.where(key < NB, 2 * base + before, 2 * NPAIR)
-    hit = jnp.arange(2 * NPAIR, dtype=jnp.int32)[:, None] == place[None, :]
-    slot = NS - jnp.sum(jnp.where(hit, NS - slots[None, :], 0), axis=1)
-    colm = jnp.sum(jnp.where(hit, block_index[None, :, 1], 0), axis=1)
-    opens = jnp.any(jnp.arange(NPAIR, dtype=jnp.int32)[:, None] == start[None, :NB], axis=1)
-    keep = 1.0 - opens.astype(F32)
-    last = start[1:] - 1
-    return slot.astype(jnp.int32), colm.astype(jnp.int32), keep, last.astype(jnp.int32)
+    )(live, index, shared, tmat, mass)
 
 
 def body(tmat, stored_mass_blocks, block_index, live_block_count, send_rows):
-    slot, colm, keep, last = plan(block_index, live_block_count)
-    idx = jnp.broadcast_to(send_rows.reshape(4 * BS, 1), (4 * BS, BS))
-    return couple(slot, colm, keep, last, idx, tmat, stored_mass_blocks)
+    return couple(live_block_count, block_index, send_rows, tmat, stored_mass_blocks)
 
 
 def solution(mesh):

time: 92.8 us -> 88.7 us (0.956); the launches traced: 91.5 us -> 88.5 us
  other arithmetic: 3.94 us -> 0 us
  Pallas kernels: 84 us -> 85 us
    sub x3 -> x0, other arithmetic: 1.85 us -> none  [the longest x1 0.66 us: plan(): last = start[1:] - 1]
    reduce_sum x5 -> x0, other arithmetic: 1.22 us -> none  [the longest x1 0.74 us: plan(): colm = jnp.sum(jnp.where(hit, block_index[None, :, 1], 0), axis=1)]
    pallas_call x1, Pallas kernels: 84 us -> 85 us  [couple(): pl.pallas_call(couple_kernel, out_shape=jax.ShapeDtypeStruct((16, W), F32...]
where the time goes in v3:
time: 88.7 us; the launch traced here: 88.5 us
  Pallas kernels  85 us (96%)
  local copies, waits for them, and re-layouts  2.83 us (3%)
    pallas_call x1, Pallas kernels, couple(): pl.pallas_call(couple_kernel, out_shape=jax.ShapeDtypeStruct((16, W), F32...  85 us
    unnamed x2, local copies, waits for them, and re-layouts  2.83 us

profile of v3, /device:TPU:33, one launch (start us, length us, event | category | flops | bytes accessed | tf_op | source)
XLA Modules:
  0.0 88.5 jit_solution(7372733433912193550)
XLA Ops:
  0.7 1.5 %copy.6.index_ref = s32[256,2]{1,0:T(8,128)} copy(s32[256,2]{0,1:T(2,128)} %param.7) | data formatting | bytes 4096 | tf_op args[2]
  2.1 85.0 %couple.1 = f32[16,512]{1,0:T(8,128)} custom-call(s32[1]{0:T(128)S(6)} %copy.8.live_ref, s32[256,2]{1,0:T(8,128)} %copy.6.index_ref, s32[2,256]{1,0:T(2,128)} %shared_ref.1, bf16[4096,512]{1,0:T(8,128)(2,1)} %tmat_hbm.1, bf16[256,128,128]{2,1,0:T(8,128)(2,1)} %mass_hbm.1), custom_call_target="tpu_custom_call" | custom-call | tf_op jit(solution)/shard_map/couple/pallas_call | solution.py:487
  87.1 1.4 %copy.9 = f32[16,512]{1,0:T(8,128)} copy(f32[16,512]{1,0:T(8,128)} %couple.1) | data formatting | bytes 65536

commit v4 on v3

--- a/solution.py
+++ b/solution.py
@@ -159,11 +159,14 @@
             steps[k * unr + u, :, :n * MC] = total.astype(BF16)
         acc[:, :n * MC] = total
 
-    def turn(n, first, r):
-        done = lax.dot_general(
+    def turned_block(n, r):
+        return lax.dot_general(
             eye[:n * MC, :n * MC], steps[order[3, r], :, :n * MC], (((1,), (1,)), ((), ())),
             preferred_element_type=F32,
         ).astype(BF16)
+
+    def turn(n, first, r):
+        done = turned_block(n, r)
         for v in range(n):
             xt[first + v, r] = done[v * MC:(v + 1) * MC]
 
@@ -267,25 +270,28 @@
         def _():
             to_lower().start()
 
-        def arrange(n, first, b):
-            rows = tmat[pl.ds(pl.multiple_of(b * BS, BS), BS), :]
-            turned = jnp.dot(rows, perm[:, first * MC:(first + n) * MC], preferred_element_type=F32).astype(BF16)
-            for v in range(n):
-                ext[first + v, b] = turned[:, v * MC:(v + 1) * MC]
-
-        def send_raw(i):
+        def trio(i, make, store):
+            blocks = [FIRST[0] + i, FIRST[1] + i, jnp.minimum(FIRST[2] + i, NB - 1)]
+            made = make(blocks)
             for t in range(3):
                 @pl.when(i < FIRST[t + 1] - FIRST[t])
                 def _():
-                    arrange(1, 0, FIRST[t] + i)
-                    from_root(0, t, 0, FIRST[t] + i)
-
-        def arrange_four(n, first, i):
-            for u in range(4):
-                arrange(n, first, 4 * i + u)
+                    store(t, blocks[t], made[t])
+
+        def send_raw(i):
+            def make(blocks):
+                rows = jnp.concatenate([tmat[pl.ds(pl.multiple_of(b * BS, BS), BS), :] for b in blocks], axis=0)
+                turned = jnp.dot(rows, perm[...], preferred_element_type=F32).astype(BF16)
+                return [turned[t * BS:(t + 1) * BS] for t in range(3)]
+
+            def store(t, b, turned):
+                for j in range(NCH):
+                    ext[j, b] = turned[:, j * MC:(j + 1) * MC]
+                from_root(0, t, 0, b)
+
+            trio(i, make, store)
 
         loop(PER, send_raw)
-        loop(NB // 4, functools.partial(arrange_four, 1, 1))
         mass_load.wait()
 
         @pl.when(dom > 0)
@@ -313,21 +319,31 @@
             loop(NPAIR // unr, functools.partial(mass_step, n, first, unr))
 
         def send_mass(n, first, j, i):
+            def store(t, b, done):
+                for v in range(n):
+                    xt[first + v, b] = done[v * MC:(v + 1) * MC]
+                from_root(2, t, j, b)
+
+            trio(i, lambda blocks: [turned_block(n, b) for b in blocks], store)
+
+        def send_last(i):
             for t in range(3):
                 @pl.when(i < FIRST[t + 1] - FIRST[t])
                 def _():
-                    if n:
-                        turn(n, first, FIRST[t] + i)
-                    from_root(2, t, j, FIRST[t] + i)
+                    from_root(2, t, 2, FIRST[t] + i)
 
         product(1, 1, 16)
         loop(PER, functools.partial(send_mass, 1, 1, 0))
-        loop(NB // 4, functools.partial(arrange_four, 2, 2))
         product(2, 2, 8)
         loop(PER, functools.partial(send_mass, 2, 2, 1))
-        loop(PER, functools.partial(send_mass, 0, 2, 2))
+        loop(PER, send_last)
         product(1, 0, 16)
-        loop(NB, functools.partial(turn, 1, 0))
+
+        def turn_four(i):
+            for u in range(4):
+                turn(1, 0, 4 * i + u)
+
+        loop(NB // 4, turn_four)
         accs[...] = jnp.zeros_like(accs)
 
         def reduce_chunk(j):

time: 88.7 us -> 80 us (0.902)
  Pallas kernels: 85 us -> 76.3 us
    pallas_call x1, Pallas kernels: 85 us -> 76.3 us  [couple(): pl.pallas_call(couple_kernel, out_shape=jax.ShapeDtypeStruct((16, W), F32...]
where the time goes in v4:
time: 80 us; the launch traced here: 79.8 us
  Pallas kernels  76.3 us (95%)
  local copies, waits for them, and re-layouts  2.83 us (4%)
    pallas_call x1, Pallas kernels, couple(): pl.pallas_call(couple_kernel, out_shape=jax.ShapeDtypeStruct((16, W), F32...  76.3 us
    unnamed x2, local copies, waits for them, and re-layouts  2.83 us

profile of v4, /device:TPU:33, one launch (start us, length us, event | category | flops | bytes accessed | tf_op | source)
XLA Modules:
  0.0 79.8 jit_solution(12258604453375423932)
XLA Ops:
  0.7 1.5 %copy.6.index_ref = s32[256,2]{1,0:T(8,128)} copy(s32[256,2]{0,1:T(2,128)} %param.7) | data formatting | bytes 4096 | tf_op args[2]
  2.1 76.3 %couple.1 = f32[16,512]{1,0:T(8,128)} custom-call(s32[1]{0:T(128)S(6)} %copy.8.live_ref, s32[256,2]{1,0:T(8,128)} %copy.6.index_ref, s32[2,256]{1,0:T(2,128)} %shared_ref.1, bf16[4096,512]{1,0:T(8,128)(2,1)} %tmat_hbm.1, bf16[256,128,128]{2,1,0:T(8,128)(2,1)} %mass_hbm.1), custom_call_target="tpu_custom_call" | custom-call | tf_op jit(solution)/shard_map/couple/pallas_call | solution.py:503
  78.4 1.4 %copy.9 = f32[16,512]{1,0:T(8,128)} copy(f32[16,512]{1,0:T(8,128)} %couple.1) | data formatting | bytes 65536

commit v5 on v4

--- a/solution.py
+++ b/solution.py
@@ -244,10 +244,11 @@
                 accs[h] += got[h * BS:(h + 1) * BS]
 
         loop(NB // 8, gather)
+        got = jnp.concatenate([accs[h].astype(BF16) for h in range(4)], axis=0)
+        got = jnp.dot(got, perm[...], preferred_element_type=F32).astype(BF16)
         for h in range(4):
-            got = jnp.dot(accs[h].astype(BF16), perm[...], preferred_element_type=F32).astype(BF16)
             for j in range(NCH):
-                lists[j, h] = got[:, j * MC:(j + 1) * MC]
+                lists[j, h] = got[h * BS:(h + 1) * BS, j * MC:(j + 1) * MC]
 
         pl.semaphore_wait(barrier, 20)
         def to_upper():
@@ -332,9 +333,9 @@
                 def _():
                     from_root(2, t, 2, FIRST[t] + i)
 
-        product(1, 1, 16)
+        product(1, 1, 24)
         loop(PER, functools.partial(send_mass, 1, 1, 0))
-        product(2, 2, 8)
+        product(2, 2, 12)
         loop(PER, functools.partial(send_mass, 2, 2, 1))
         loop(PER, send_last)
         product(1, 0, 16)

time: 80 us -> 79.7 us (level)
  no operation moved by 1% of the time
where the time goes in v5:
time: 79.7 us; the launch traced here: 79.5 us
  Pallas kernels  76 us (95%)
  local copies, waits for them, and re-layouts  2.83 us (4%)
    pallas_call x1, Pallas kernels, couple(): pl.pallas_call(couple_kernel, out_shape=jax.ShapeDtypeStruct((16, W), F32...  76 us
    unnamed x2, local copies, waits for them, and re-layouts  2.83 us

profile of v5, /device:TPU:33, one launch (start us, length us, event | category | flops | bytes accessed | tf_op | source)
XLA Modules:
  0.0 79.5 jit_solution(10221379933938450325)
XLA Ops:
  0.7 1.5 %copy.6.index_ref = s32[256,2]{1,0:T(8,128)} copy(s32[256,2]{0,1:T(2,128)} %param.7) | data formatting | bytes 4096 | tf_op args[2]
  2.1 76.0 %couple.1 = f32[16,512]{1,0:T(8,128)} custom-call(s32[1]{0:T(128)S(6)} %copy.8.live_ref, s32[256,2]{1,0:T(8,128)} %copy.6.index_ref, s32[2,256]{1,0:T(2,128)} %shared_ref.1, bf16[4096,512]{1,0:T(8,128)(2,1)} %tmat_hbm.1, bf16[256,128,128]{2,1,0:T(8,128)(2,1)} %mass_hbm.1), custom_call_target="tpu_custom_call" | custom-call | tf_op jit(solution)/shard_map/couple/pallas_call | solution.py:504
  78.1 1.4 %copy.9 = f32[16,512]{1,0:T(8,128)} copy(f32[16,512]{1,0:T(8,128)} %couple.1) | data formatting | bytes 65536

commit v6 on v5

--- a/solution.py
+++ b/solution.py
@@ -440,7 +440,11 @@
         loop(T_END + 4 * OFF, tick)
 
     last = NCH - 1
-    loop(8, functools.partial(contract, last))
+    whole = jnp.zeros((MC, W), F32)
+    for i in range(4):
+        lhs = jnp.concatenate([xt[last, 8 * i + u] for u in range(8)], axis=1)
+        whole = whole + jnp.dot(lhs, tmat[i * 1024:(i + 1) * 1024, :], preferred_element_type=F32)
+    accs[last] = whole
     hand_over(last)
 
     @pl.when(jnp.logical_not(root))

time: 79.7 us -> 79.1 us (level)
  no operation moved by 1% of the time
where the time goes in v6:
time: 79.1 us; the launch traced here: 78.9 us
  Pallas kernels  75.4 us (95%)
  local copies, waits for them, and re-layouts  2.83 us (4%)
    pallas_call x1, Pallas kernels, couple(): pl.pallas_call(couple_kernel, out_shape=jax.ShapeDtypeStruct((16, W), F32...  75.4 us
    unnamed x2, local copies, waits for them, and re-layouts  2.83 us

profile of v6, /device:TPU:33, one launch (start us, length us, event | category | flops | bytes accessed | tf_op | source)
XLA Modules:
  0.0 78.9 jit_solution(8866479575775962621)
XLA Ops:
  0.7 1.5 %copy.6.index_ref = s32[256,2]{1,0:T(8,128)} copy(s32[256,2]{0,1:T(2,128)} %param.7) | data formatting | bytes 4096 | tf_op args[2]
  2.1 75.4 %couple.1 = f32[16,512]{1,0:T(8,128)} custom-call(s32[1]{0:T(128)S(6)} %copy.8.live_ref, s32[256,2]{1,0:T(8,128)} %copy.6.index_ref, s32[2,256]{1,0:T(2,128)} %shared_ref.1, bf16[4096,512]{1,0:T(8,128)(2,1)} %tmat_hbm.1, bf16[256,128,128]{2,1,0:T(8,128)(2,1)} %mass_hbm.1), custom_call_target="tpu_custom_call" | custom-call | tf_op jit(solution)/shard_map/couple/pallas_call | solution.py:508
  77.5 1.4 %copy.9 = f32[16,512]{1,0:T(8,128)} copy(f32[16,512]{1,0:T(8,128)} %couple.1) | data formatting | bytes 65536

commit v7 on v6

--- a/solution.py
+++ b/solution.py
@@ -175,6 +175,11 @@
         rhs = tmat[pl.ds(pl.multiple_of(i * 512, 512), 512), :]
         accs[j] += jnp.dot(lhs, rhs, preferred_element_type=F32)
 
+    def contract_wide(j, i):
+        lhs = jnp.concatenate([xt[j, 8 * i + u] for u in range(8)], axis=1)
+        rhs = tmat[pl.ds(pl.multiple_of(i * 1024, 1024), 1024), :]
+        accs[j] += jnp.dot(lhs, rhs, preferred_element_type=F32)
+
     def pair_copy(j):
         return pltpu.make_async_remote_copy(
             src_ref=accs.at[j], dst_ref=pairbuf.at[j // 2],
@@ -348,7 +353,7 @@
         accs[...] = jnp.zeros_like(accs)
 
         def reduce_chunk(j):
-            loop(8, functools.partial(contract, j))
+            loop(4, functools.partial(contract_wide, j))
             hand_over(j)
 
             @pl.when(j > 0)
@@ -413,9 +418,9 @@
             def _():
                 mass_step(1, 0, 8, m)
 
-            @pl.when((m >= 12) & (m < 20))
-            def _():
-                contract(1, m - 12)
+            @pl.when((m >= 12) & (m < 16))
+            def _():
+                contract_wide(1, m - 12)
 
             @pl.when((m >= 18) & (m < 26))
             def _():
@@ -424,9 +429,9 @@
                     turn(1, 0, 4 * i + u)
                 contract(0, i)
 
-            @pl.when((m >= 23) & (m < 31))
-            def _():
-                contract(2, m - 23)
+            @pl.when((m >= 26) & (m < 30))
+            def _():
+                contract_wide(2, m - 26)
 
             for j, at in ((1, 20), (0, 26), (2, 31)):
                 @pl.when(m == at)

time: 79.1 us -> 78 us (0.986)
  Pallas kernels: 75.4 us -> 74.2 us
    pallas_call x1, Pallas kernels: 75.4 us -> 74.2 us  [couple(): pl.pallas_call(couple_kernel, out_shape=jax.ShapeDtypeStruct((16, W), F32...]
where the time goes in v7:
time: 78 us; the launch traced here: 77.7 us
  Pallas kernels  74.2 us (95%)
  local copies, waits for them, and re-layouts  2.83 us (4%)
    pallas_call x1, Pallas kernels, couple(): pl.pallas_call(couple_kernel, out_shape=jax.ShapeDtypeStruct((16, W), F32...  74.2 us
    unnamed x2, local copies, waits for them, and re-layouts  2.83 us

profile of v7, /device:TPU:33, one launch (start us, length us, event | category | flops | bytes accessed | tf_op | source)
XLA Modules:
  0.0 77.7 jit_solution(6486335907793548452)
XLA Ops:
  0.7 1.5 %copy.6.index_ref = s32[256,2]{1,0:T(8,128)} copy(s32[256,2]{0,1:T(2,128)} %param.7) | data formatting | bytes 4096 | tf_op args[2]
  2.1 74.2 %couple.1 = f32[16,512]{1,0:T(8,128)} custom-call(s32[1]{0:T(128)S(6)} %copy.8.live_ref, s32[256,2]{1,0:T(8,128)} %copy.6.index_ref, s32[2,256]{1,0:T(2,128)} %shared_ref.1, bf16[4096,512]{1,0:T(8,128)(2,1)} %tmat_hbm.1, bf16[256,128,128]{2,1,0:T(8,128)(2,1)} %mass_hbm.1), custom_call_target="tpu_custom_call" | custom-call | tf_op jit(solution)/shard_map/couple/pallas_call | solution.py:513
  76.4 1.4 %copy.9 = f32[16,512]{1,0:T(8,128)} copy(f32[16,512]{1,0:T(8,128)} %couple.1) | data formatting | bytes 65536
